TPU v7x, 32 devices: a whole 2x2x4 slice. The times are simulated.
32 devices in a mesh: dp: 8 (over z, x), head: 4 (over y, core).
Axes of the slice: x: 2, y: 2, z: 4, core: 2. Of those that a mesh axis runs over, the one named last changes fastest.
Arguments:
- hidden_in: bfloat16 [8192, 2048], P(('dp', 'head')), may hold values from -6 to 6
- in_gain: float32 [2048], replicated, may hold values from 0.1 to 1.9
- gate_proj: bfloat16 [2048, 4096], P(None, 'head'), may hold values from -0.125 to 0.125
- value_proj: bfloat16 [2048, 4096], P(None, 'head'), may hold values from -0.125 to 0.125
- state_proj: bfloat16 [2048, 256], replicated, may hold values from -0.125 to 0.125
- step_proj: bfloat16 [2048, 64], P(None, 'head'), may hold values from -0.03125 to 0.03125
- conv_value: float32 [4, 4096], P(None, 'head'), may hold values from -3 to 3
- conv_value_bias: float32 [4096], P('head'), may hold values from -3 to 3
- conv_state: float32 [4, 256], replicated, may hold values from -3 to 3
- conv_state_bias: float32 [256], replicated, may hold values from -3 to 3
- step_bias: float32 [64], P('head'), may hold values from -6 to -1
- decay_log: float32 [64], P('head'), may hold values from 0 to 2.77
- skip_gain: float32 [64], P('head'), may hold values from 0.5 to 1.5
- out_gain: float32 [4096], P('head'), may hold values from 0.1 to 1.9
- out_proj: bfloat16 [4096, 2048], P('head'), may hold values from -0.125 to 0.125
- cotangent: bfloat16 [8192, 2048], P(('dp', 'head')), may hold values from -6 to 6
- width_level: int32 [8], P('dp'), may hold values from 0 to 3
Outputs:
- block_out: bfloat16 [8192, 2048], P(('dp', 'head'))
- in_grad: float32 [8192, 2048], P(('dp', 'head'))
- in_gain_grad: float32 [2048], replicated
- gate_proj_grad: float32 [2048, 4096], P('dp', 'head')
- value_proj_grad: float32 [2048, 4096], P('dp', 'head')
- state_proj_grad: float32 [2048, 256], P('dp')
- step_proj_grad: float32 [2048, 64], P('dp', 'head')
- conv_value_grad: float32 [4, 4096], P(None, 'head')
- conv_value_bias_grad: float32 [4096], P('head')
- conv_state_grad: float32 [4, 256], replicated
- conv_state_bias_grad: float32 [256], replicated
- step_bias_grad: float32 [64], P('head')
- decay_log_grad: float32 [64], P('head')
- skip_gain_grad: float32 [64], P('head')
- out_gain_grad: float32 [4096], P('head')
- out_proj_grad: float32 [4096, 2048], P('head', 'dp')
All inputs are finite; a program needn't handle non-finite values.
Results may differ from a plain program's by a relative error of at most 0.0079.
Values may be sent and summed in bfloat16 or wider, within the bound.
A program may use at most 192 MiB of HBM per device.

v0:
```python
import jax
import jax.numpy as jnp
from jax import lax
from jax.sharding import PartitionSpec as P

SPAN = 256
HIGH = lax.Precision.HIGHEST
EPS = 1e-05


def conv_causal(series, kernel, shift):
    kernel_len = kernel.shape[0]
    length = series.shape[0]
    padded = jnp.pad(series, ((kernel_len - 1, 0), (0, 0)))
    running = shift[None, :] + kernel[0][None, :] * padded[0:length]
    for offset in range(1, kernel_len):
        running = running + kernel[offset][None, :] * padded[offset : offset + length]
    return running


def state_space(inputs, step_size, decay_rate, key_rows, query_rows, skip_gain):
    seq_len, heads, head_dim = inputs.shape
    blocks = seq_len // SPAN
    values = inputs.reshape(blocks, SPAN, heads, head_dim)
    deltas = step_size.reshape(blocks, SPAN, heads)
    keys = key_rows.reshape(blocks, SPAN, -1)
    queries = query_rows.reshape(blocks, SPAN, -1)
    cumul = jnp.cumsum(deltas * decay_rate[None, None, :], axis=1)
    inner = jnp.einsum("cin,cjn->cij", queries, keys, precision=HIGH)
    lower = (jnp.arange(SPAN)[:, None] >= jnp.arange(SPAN)[None, :])[None, :, :, None]
    spread = cumul[:, :, None, :] - cumul[:, None, :, :]
    mixing = jnp.where(lower, jnp.exp(jnp.where(lower, spread, 0.0)), 0.0) * inner[:, :, :, None]
    scaled = values * deltas[:, :, :, None]
    within = jnp.einsum("cijh,cjhp->cihp", mixing, scaled, precision=HIGH)
    tails = jnp.exp(cumul[:, -1:, :] - cumul)
    states = jnp.einsum("cjhp,cjn->chpn", scaled * tails[:, :, :, None], keys, precision=HIGH)
    totals = jnp.exp(cumul[:, -1, :])

    def carry_state(state, item):
        fresh, factor = item
        return (factor[:, None, None] * state + fresh, state)

    start = jnp.zeros((heads, head_dim, keys.shape[2]), dtype=inputs.dtype)
    _, entering = lax.scan(carry_state, start, (states, totals))
    across = (
        jnp.einsum("cin,chpn->cihp", queries, entering, precision=HIGH)
        * jnp.exp(cumul)[:, :, :, None]
    )
    result = within + across + values * skip_gain[None, None, :, None]
    return result.reshape(seq_len, heads, head_dim)


def mix_block(
    value_pre,
    state_pre,
    step_pre,
    gate_pre,
    conv_value,
    conv_value_bias,
    conv_state,
    conv_state_bias,
    step_bias,
    decay_log,
    skip_gain,
    keep,
):
    seq_len = value_pre.shape[0]
    heads = step_pre.shape[1]
    value_act = jax.nn.silu(conv_causal(value_pre, conv_value, conv_value_bias))
    state_act = jax.nn.silu(conv_causal(state_pre, conv_state, conv_state_bias))
    half = state_act.shape[1] // 2
    step_size = jax.nn.softplus(step_pre + step_bias[None, :])
    inputs = value_act.reshape(seq_len, heads, -1) * keep[None, :, None]
    result = state_space(
        inputs, step_size, -jnp.exp(decay_log), state_act[:, :half], state_act[:, half:], skip_gain
    )
    return result.reshape(seq_len, -1) * jax.nn.silu(gate_pre)


def contract_rows(left, right):
    return lax.dot_general(
        left, right, (((0,), (0,)), ((), ())), preferred_element_type=jnp.float32
    )


def contract_cols(left, right):
    return lax.dot_general(
        left, right, (((1,), (1,)), ((), ())), preferred_element_type=jnp.float32
    )


def per_device(
    hidden_in,
    in_gain,
    gate_proj,
    value_proj,
    state_proj,
    step_proj,
    conv_value,
    conv_value_bias,
    conv_state,
    conv_state_bias,
    step_bias,
    decay_log,
    skip_gain,
    out_gain,
    out_proj,
    cotangent,
    width_level,
):
    heads_here = step_bias.shape[0]
    head_dim = conv_value.shape[1] // heads_here
    groups = lax.axis_size("head")
    rank = lax.axis_index("head")
    rows_own = hidden_in.shape[0]
    seqs = width_level.shape[0]
    resid = hidden_in.astype(jnp.float32)
    in_scale = lax.rsqrt(jnp.mean(resid * resid, axis=-1, keepdims=True) + EPS)
    normed = (resid * in_scale * in_gain).astype(jnp.bfloat16)
    whole = lax.all_gather(normed, "head", axis=0, tiled=True)
    rows_all = whole.shape[0]
    seq_len = rows_all // seqs
    gate_pre = jnp.dot(whole, gate_proj, preferred_element_type=jnp.float32)
    value_pre = jnp.dot(whole, value_proj, preferred_element_type=jnp.float32)
    state_pre = jnp.dot(whole, state_proj, preferred_element_type=jnp.float32)
    step_pre = jnp.dot(whole, step_proj, preferred_element_type=jnp.float32)
    active = jnp.right_shift(heads_here, 3 - width_level)
    keep = (jnp.arange(heads_here)[None, :] < active[:, None]).astype(jnp.float32)
    seq_count = (active * groups * head_dim).astype(jnp.float32)
    token_count = jnp.broadcast_to(seq_count[:, None], (seqs, seq_len)).reshape(rows_all)
    params = (
        conv_value,
        conv_value_bias,
        conv_state,
        conv_state_bias,
        step_bias,
        decay_log,
        skip_gain,
    )

    def group_mix(value_in, state_in, step_in, gate_in, *weights):

        def split(array):
            return array.reshape(seqs, seq_len, array.shape[1])

        mapped = jax.vmap(
            mix_block, in_axes=(0, 0, 0, 0, None, None, None, None, None, None, None, 0)
        )
        result = mapped(
            split(value_in), split(state_in), split(step_in), split(gate_in), *weights, keep
        )
        return result.reshape(rows_all, -1)

    gated = group_mix(value_pre, state_pre, step_pre, gate_pre, *params)
    squares = lax.psum(jnp.sum(gated * gated, axis=-1), "head")
    out_scale = lax.rsqrt(squares / token_count + EPS)[:, None]
    normed_out = (gated * out_scale * out_gain).astype(jnp.bfloat16)
    own_out = lax.psum_scatter(
        jnp.dot(normed_out, out_proj, preferred_element_type=jnp.float32),
        "head",
        scatter_dimension=0,
        tiled=True,
    )
    block_out = (resid + own_out).astype(jnp.bfloat16)
    cot_all = lax.all_gather(cotangent, "head", axis=0, tiled=True)
    out_proj_part = contract_rows(normed_out, cot_all)
    d_normed_out = contract_cols(cot_all, out_proj)
    weighted = d_normed_out * out_gain
    stat = lax.psum(jnp.sum(weighted * gated, axis=-1), "head")
    d_gated = weighted * out_scale - gated * out_scale**3 * (stat / token_count)[:, None]
    out_gain_part = jnp.sum(d_normed_out * gated * out_scale, axis=0)
    _, pull = jax.vjp(group_mix, value_pre, state_pre, step_pre, gate_pre, *params)
    (
        d_value_pre,
        d_state_pre,
        d_step_pre,
        d_gate_pre,
        g_conv_value,
        g_conv_value_bias,
        g_conv_state,
        g_conv_state_bias,
        g_step_bias,
        g_decay_log,
        g_skip_gain,
    ) = pull(d_gated)
    d_state_pre, g_conv_state, g_conv_state_bias = lax.psum(
        (d_state_pre, g_conv_state, g_conv_state_bias), "head"
    )
    d_gate_low = d_gate_pre.astype(jnp.bfloat16)
    d_value_low = d_value_pre.astype(jnp.bfloat16)
    d_state_low = d_state_pre.astype(jnp.bfloat16)
    d_step_low = d_step_pre.astype(jnp.bfloat16)
    d_normed = lax.psum_scatter(
        contract_cols(d_gate_low, gate_proj)
        + contract_cols(d_value_low, value_proj)
        + contract_cols(d_step_low, step_proj),
        "head",
        scatter_dimension=0,
        tiled=True,
    )
    state_own = lax.dynamic_slice_in_dim(d_state_low, rank * rows_own, rows_own, 0)
    d_normed = d_normed + contract_cols(state_own, state_proj)
    gate_part = contract_rows(whole, d_gate_low)
    value_part = contract_rows(whole, d_value_low)
    state_part = contract_rows(whole, d_state_low)
    step_part = contract_rows(whole, d_step_low)
    scaled_grad = d_normed * in_gain
    in_grad = (
        cotangent.astype(jnp.float32)
        + scaled_grad * in_scale
        - resid
        * in_scale**3
        * jnp.sum(scaled_grad * resid, axis=-1, keepdims=True)
        / resid.shape[1]
    )
    in_gain_grad = lax.psum(jnp.sum(d_normed * resid * in_scale, axis=0), ("dp", "head"))
    (
        conv_value_grad,
        conv_value_bias_grad,
        step_bias_grad,
        decay_log_grad,
        skip_gain_grad,
        out_gain_grad,
        conv_state_grad,
        conv_state_bias_grad,
    ) = lax.psum(
        (
            g_conv_value,
            g_conv_value_bias,
            g_step_bias,
            g_decay_log,
            g_skip_gain,
            out_gain_part,
            g_conv_state,
            g_conv_state_bias,
        ),
        "dp",
    )
    gate_proj_grad, value_proj_grad, state_proj_grad, step_proj_grad, out_proj_grad = (
        lax.psum_scatter(gate_part, "dp", scatter_dimension=0, tiled=True),
        lax.psum_scatter(value_part, "dp", scatter_dimension=0, tiled=True),
        lax.psum_scatter(state_part, "dp", scatter_dimension=0, tiled=True),
        lax.psum_scatter(step_part, "dp", scatter_dimension=0, tiled=True),
        lax.psum_scatter(out_proj_part, "dp", scatter_dimension=1, tiled=True),
    )
    return (
        block_out,
        in_grad,
        in_gain_grad,
        gate_proj_grad,
        value_proj_grad,
        state_proj_grad,
        step_proj_grad,
        conv_value_grad,
        conv_value_bias_grad,
        conv_state_grad,
        conv_state_bias_grad,
        step_bias_grad,
        decay_log_grad,
        skip_gain_grad,
        out_gain_grad,
        out_proj_grad,
    )


def solution(mesh):
    placed = (
        P(("dp", "head"), None),
        P(),
        P(None, "head"),
        P(None, "head"),
        P(),
        P(None, "head"),
        P(None, "head"),
        P("head"),
        P(),
        P(),
        P("head"),
        P("head"),
        P("head"),
        P("head"),
        P("head", None),
        P(("dp", "head"), None),
        P("dp"),
    )
    return jax.shard_map(
        per_device,
        mesh=mesh,
        in_specs=placed,
        out_specs=(
            P(("dp", "head"), None),
            P(("dp", "head"), None),
            P(),
            P("dp", "head"),
            P("dp", "head"),
            P("dp", None),
            P("dp", "head"),
            P(None, "head"),
            P("head"),
            P(),
            P(),
            P("head"),
            P("head"),
            P("head"),
            P("head"),
            P("head", "dp"),
        ),
        check_vma=False,
    )
```

profile of v0, /device:TPU:0, one launch (start us, length us, event | category | flops | bytes accessed | tf_op | source)
XLA Modules:
  0.0 1183.8 jit_solution(4698405417298480208)
XLA Ops:
  15.4 33.9 %all-gather.3.cloned.1.call-done = bf16[1024,2048]{1,0:T(8,128)(2,1)} async-done(((bf16[256,2048]{1,0:T(8,128)(2,1)}), bf16[1024,2048]{1,0:T(8,128)(2,1)}) %all-gather.3.cloned.1.call-update) | async-done | bytes 4194320 | tf_op jit(solution)/shard_map/all_gather | solution.py:120
  114.1 20.4 %fusion.9 = f32[4,16,64,256]{3,2,1,0:T(8,128)} fusion(f32[4,256,256]{2,1,0:T(8,128)S(1)} %copy-done.20, f32[4,256,16]{1,2,0:T(8,128)S(1)} %copy-done.30, pred[256,256]{1,0:T(8,128)(4,1)S(1)} %copy-done.28, f32[4,256,16,64]{1,3,2,0:T(8,128)S(1)} %copy-done.4, f32[4,256,16]{1,2,0:T(8,128)S(1)} %bitcast.318, f32[16]{0:T(128)S(1)} %copy-done.57), kind=kOutput, calls=%fused_computation.25 | convolution fusion | flops 3240099840 | bytes 9633856 | tf_op jit(solution)/shard_map/vmap(cijh,cjhp->cihp)/dot_general | solution.py:34
  144.3 10.0 fusion.31
  170.1 12.6 %multiply_reduce_fusion.8 = (f32[1024]{0:T(1024)S(1)}, f32[1024,1024]{1,0:T(8,128)}, f32[1024,1024]{1,0:T(8,128)}) fusion(f32[1024,1024]{1,0:T(8,128)} %reshape.750, bf16[1024,2048]{1,0:T(8,128)(2,1)} %all-gather.3.cloned.1.call-done, bf16[2048,1024]{1,0:T(8,128)(2,1)} %param.25), kind=kOutput, calls=%fused_computation.79 | convolution fusion | flops 4302306304 | bytes 20975616 | tf_op jit(solution)/shard_map/dot_general | solution.py:123
  188.6 11.9 %multiply_reduce_fusion = (f32[1024]{0:T(1024)}, f32[1024]{0:T(1024)S(1)}, f32[1024,1024]{1,0:T(8,128)}) fusion(f32[1024,1024]{1,0:T(8,128)} %get-tuple-element.489, f32[1024]{0:T(1024)S(1)} %get-tuple-element.487, f32[1024]{0:T(1024)S(1)} %copy-done.22, bf16[1024,2048]{1,0:T(8,128)(2,1)} %all-gather.5.cloned.1.call-done, bf16[1024,2048]{1,0:T(8,128)(2,1)} %param.37), kind=kOutput, calls=%fused_computation.69 | convolution fusion | flops 4301256704 | bytes 16793600 | tf_op jit(solution)/shard_map/dot_general | solution.py:87
  206.6 9.2 fusion.28
  242.3 28.4 %fusion.11 = (f32[4,256,16]{1,2,0:T(8,128)S(1)}, f32[4,256,16]{1,2,0:T(8,128)}, f32[4,256,256]{2,1,0:T(8,128)}) fusion(f32[4,256,16]{1,2,0:T(8,128)S(1)} %copy-done.31, f32[4,256,256]{2,1,0:T(8,128)} %fusion.132, pred[256,256]{1,0:T(8,128)(4,1)S(1)} %copy-done.29, f32[4,256,16,64]{1,3,2,0:T(8,128)} %copy.274, f32[4,256,16]{1,2,0:T(8,128)S(1)} %bitcast.319, ...), kind=kOutput, calls=%fused_computation.27 | convolution fusion | flops 3269165056 | bytes 10813504 | tf_op jit(solution)/shard_map/transpose(jvp(vmap(cijh,cjhp->cihp)))/dot_general | solution.py:34
  284.6 9.2 while.49
  300.9 21.0 %fusion.29 = (f32[4,256,16]{1,2,0:T(8,128)S(1)}, f32[4,256,16]{1,2,0:T(8,128)}, f32[1,4,256,16,64]{2,4,3,1,0:T(8,128)}, f32[1,4,256,16,64]{2,4,3,1,0:T(8,128)}) fusion(f32[4,16,64,256]{3,2,1,0:T(8,128)S(1)} %fusion.56, f32[1,4,256,16,64]{2,4,3,1,0:T(8,128)S(1)} %copy-done.8, f32[4,256,16]{1,2,0:T(8,128)S(1)} %bitcast.320, f32[16]{0:T(128)S(1)} %copy-done.57, ...), kind=kOutput, calls=%fused_computation.61 | convolution fusion | flops 3253698560 | bytes 35061888 | tf_op jit(solution)/shard_map/transpose(jvp(vmap(cijh,cjhp->cihp)))/dot_general | solution.py:34
  324.3 9.9 reduce-window.16
  351.6 12.2 %multiply_reduce_fusion.3 = (f32[1024]{0:T(1024)S(1)}, f32[1024]{0:T(1024)S(1)}, f32[1024]{0:T(1024)S(1)}, f32[1024]{0:T(1024)S(1)}, f32[1024]{0:T(1024)S(1)}, /*index=5*/f32[1,1024,1024]{2,1,0:T(8,128)}) fusion(f32[1,1024,1024]{2,1,0:T(8,128)} %bitcast.295, f32[1024,1024]{1,0:T(8,128)} %copy-done.2, f32[1,1024,1024]{2,1,0:T(8,128)} %get-tuple-element.493, ...), kind=kLoop, calls=%fused_computation.72 | loop fusion | flops 19917824 | bytes 20996096 | tf_op jit(solution)/shard_map/transpose(jvp(vmap()))/reduce_sum | solution.py:17
  418.8 13.0 %fusion.119 = f32[1024,2048]{1,0:T(8,128)} fusion(bf16[1024,2048]{1,0:T(8,128)(2,1)} %param.37, f32[1024,1024]{1,0:T(8,128)} %get-tuple-element.489, f32[1024]{0:T(1024)S(1)} %copy-done.22, f32[1024]{0:T(1024)S(1)} %get-tuple-element.487), kind=kOutput, calls=%fused_computation.208 | convolution fusion | flops 4298113024 | bytes 16785408 | tf_op jit(solution)/shard_map/dot_general | solution.py:159
  441.8 10.4 fusion.80
  457.8 42.1 %all-reduce.25 = (bf16[1024,256]{1,0:T(8,128)(2,1)S(1)}, f32[4,256]{1,0:T(4,128)S(1)}, f32[256]{0:T(256)S(1)}) all-reduce(f32[1024,256]{1,0:T(8,128)S(1)} %fusion.95, f32[4,256]{1,0:T(4,128)S(1)} %pad_add_fusion.7, f32[256]{0:T(256)S(1)} %get-tuple-element.429), channel_id=1, replica_groups=mesh['dp'=8,'head'=4] {'head'}, use_global_device_ids=true, to_apply=%region_25.26 | all-reduce | flops 263424 | bytes 1583104 | tf_op jit(solution)/shard_map/psum | solution.py:186
  505.3 11.4 fusion.118
  516.7 11.4 fusion.135
  528.5 10.6 fusion.136
  540.1 38.0 %all-reduce.22 = (f32[4,1024]{1,0:T(4,128)}, f32[1024]{0:T(1024)}, f32[4,256]{1,0:T(4,128)}, f32[256]{0:T(256)}, f32[16]{0:T(128)}, /*index=5*/f32[16]{0:T(128)}, f32[16]{0:T(128)}, f32[1024]{0:T(1024)}) all-reduce(f32[4,1024]{1,0:T(4,128)S(1)} %pad_add_fusion.6, ...), channel_id=1, replica_groups=mesh['dp'=8,'head'=4] {'dp'}, use_global_device_ids=true, to_apply=%region_37.38 | all-reduce | flops 7472 | bytes 59776 | tf_op jit(solution)/shard_map/psum | solution.py:226
  581.9 36.9 %psum.101 = f32[2048]{0:T(1024)} all-reduce(f32[2048]{0:T(1024)S(1)} %get-tuple-element.424), channel_id=1, replica_groups=mesh['dp'=8,'head'=4] {'dp','head'}, use_global_device_ids=true, to_apply=%region_28.29 | all-reduce | flops 2048 | bytes 16384 | tf_op jit(solution)/shard_map/psum | solution.py:216
  623.5 24.9 %reduce-scatter.18.cloned.1.call-done = f32[256,16]{0,1:T(8,128)} async-done(((f32[2048,16]{0,1:T(8,128)}), f32[256,16]{0,1:T(8,128)}) %reduce-scatter.18.cloned.1.call-update) | async-done | bytes 16400 | tf_op jit(solution)/shard_map/reduce_scatter | solution.py:243
  648.4 70.9 %reduce-scatter.16.cloned.1.call-done = f32[256,256]{1,0:T(8,128)} async-done(((f32[2048,256]{1,0:T(8,128)}), f32[256,256]{1,0:T(8,128)}) %reduce-scatter.16.cloned.1.call-update) | async-done | bytes 262160 | tf_op jit(solution)/shard_map/reduce_scatter | solution.py:242
  719.3 152.6 %reduce-scatter.20.cloned.1.call-done = f32[1024,256]{1,0:T(8,128)} async-done(((f32[1024,2048]{1,0:T(8,128)}), f32[1024,256]{1,0:T(8,128)}) %reduce-scatter.20.cloned.1.call-update) | async-done | bytes 1048592 | tf_op jit(solution)/shard_map/reduce_scatter | solution.py:244
  871.9 152.7 %reduce-scatter.12.cloned.1.call-done = f32[256,1024]{1,0:T(8,128)} async-done(((f32[2048,1024]{1,0:T(8,128)}), f32[256,1024]{1,0:T(8,128)}) %reduce-scatter.12.cloned.1.call-update) | async-done | bytes 1048592 | tf_op jit(solution)/shard_map/reduce_scatter | solution.py:240
  1024.6 152.2 %reduce-scatter.14.cloned.1.call-done = f32[256,1024]{1,0:T(8,128)} async-done(((f32[2048,1024]{1,0:T(8,128)}), f32[256,1024]{1,0:T(8,128)}) %reduce-scatter.14.cloned.1.call-update) | async-done | bytes 1048592 | tf_op jit(solution)/shard_map/reduce_scatter | solution.py:241
  (322 shorter events, 287.0 us)
Async XLA Ops:
  7.2 50.8 %copy-start = (bf16[2048,256]{1,0:T(8,128)(2,1)S(1)}, bf16[2048,256]{1,0:T(8,128)(2,1)}, u32[]{:S(2)}) copy-start(bf16[2048,256]{1,0:T(8,128)(2,1)} %param.27) | copy-start | bytes 3145732
  7.2 42.1 %copy-start.24 = (bf16[2048,16]{0,1:T(8,128)(2,1)S(1)}, bf16[2048,16]{0,1:T(8,128)(2,1)}, u32[]{:S(2)}) copy-start(bf16[2048,16]{0,1:T(8,128)(2,1)} %param.28) | copy-start | bytes 196612
  7.2 42.1 %copy-start.62 = (f32[16]{0:T(128)S(1)}, f32[16]{0:T(128)}, u32[]{:S(2)}) copy-start(f32[16]{0:T(128)} %param.33) | copy-start | bytes 196
  7.3 42.1 %all-gather.3.cloned.1.call-start = ((), (), s32[]{:S(2)}) async-start(), calls=%async_computation.7 | async-start | bytes 5242880 | tf_op jit(solution)/shard_map/all_gather | solution.py:120
  12.0 176.6 %all-gather.5.cloned.1.call-start = ((), (), s32[]{:S(2)}) async-start(), calls=%async_computation.9 | async-start | bytes 5242880 | tf_op jit(solution)/shard_map/all_gather | solution.py:165
  12.7 565.4 %reduce-scatter.10.cloned.1.call-start = ((), (), s32[]{:S(2)}) async-start(), calls=%async_computation.10 | async-start | bytes 10485760 | tf_op jit(solution)/shard_map/reduce_scatter | solution.py:193
  14.1 39.2 %copy-start.63 = (f32[16]{0:T(128)}, f32[16]{0:T(128)S(1)}, u32[]{:S(2)}) copy-start(f32[16]{0:T(128)S(1)} %exponential_negate_fusion) | copy-start | bytes 196
  14.6 47.5 %copy-start.48 = (f32[1,256]{1,0:T(1,128)}, f32[1,256]{1,0:T(1,128)S(1)}, u32[]{:S(2)}) copy-start(f32[1,256]{1,0:T(1,128)S(1)} %get-tuple-element.518) | copy-start | bytes 3076
  14.6 47.5 %copy-start.50 = (f32[1,256]{1,0:T(1,128)}, f32[1,256]{1,0:T(1,128)S(1)}, u32[]{:S(2)}) copy-start(f32[1,256]{1,0:T(1,128)S(1)} %get-tuple-element.519) | copy-start | bytes 3076
  14.6 47.5 %copy-start.52 = (f32[1,256]{1,0:T(1,128)}, f32[1,256]{1,0:T(1,128)S(1)}, u32[]{:S(2)}) copy-start(f32[1,256]{1,0:T(1,128)S(1)} %get-tuple-element.520) | copy-start | bytes 3076
  14.6 47.5 %copy-start.54 = (f32[1,256]{1,0:T(1,128)}, f32[1,256]{1,0:T(1,128)S(1)}, u32[]{:S(2)}) copy-start(f32[1,256]{1,0:T(1,128)S(1)} %get-tuple-element.521) | copy-start | bytes 3076
  15.4 55.8 %copy-start.32 = (f32[1,1024]{1,0:T(1,128)}, f32[1,1024]{1,0:T(1,128)S(1)}, u32[]{:S(2)}) copy-start(f32[1,1024]{1,0:T(1,128)S(1)} %get-tuple-element.514) | copy-start | bytes 12292
  15.4 55.8 %copy-start.34 = (f32[1,1024]{1,0:T(1,128)}, f32[1,1024]{1,0:T(1,128)S(1)}, u32[]{:S(2)}) copy-start(f32[1,1024]{1,0:T(1,128)S(1)} %get-tuple-element.515) | copy-start | bytes 12292
  15.4 55.8 %copy-start.36 = (f32[1,1024]{1,0:T(1,128)}, f32[1,1024]{1,0:T(1,128)S(1)}, u32[]{:S(2)}) copy-start(f32[1,1024]{1,0:T(1,128)S(1)} %get-tuple-element.516) | copy-start | bytes 12292
  15.4 55.8 %copy-start.38 = (f32[1,1024]{1,0:T(1,128)}, f32[1,1024]{1,0:T(1,128)S(1)}, u32[]{:S(2)}) copy-start(f32[1,1024]{1,0:T(1,128)S(1)} %get-tuple-element.517) | copy-start | bytes 12292
  418.6 200.3 %reduce-scatter.8.cloned.1.call-start = ((), (), s32[]{:S(2)}) async-start(), calls=%async_computation.8 | async-start | bytes 10485760 | tf_op jit(solution)/shard_map/reduce_scatter | solution.py:158
  431.8 216.6 %reduce-scatter.18.cloned.1.call-start = ((), (), s32[]{:S(2)}) async-start(), calls=%async_computation.14 | async-start | bytes 147456 | tf_op jit(solution)/shard_map/reduce_scatter | solution.py:243
  457.7 261.6 %reduce-scatter.16.cloned.1.call-start = ((), (), s32[]{:S(2)}) async-start(), calls=%async_computation.13 | async-start | bytes 2359296 | tf_op jit(solution)/shard_map/reduce_scatter | solution.py:242
  505.0 366.9 %reduce-scatter.20.cloned.1.call-start = ((), (), s32[]{:S(2)}) async-start(), calls=%async_computation.15 | async-start | bytes 9437184 | tf_op jit(solution)/shard_map/reduce_scatter | solution.py:244
  516.7 507.9 %reduce-scatter.12.cloned.1.call-start = ((), (), s32[]{:S(2)}) async-start(), calls=%async_computation.11 | async-start | bytes 9437184 | tf_op jit(solution)/shard_map/reduce_scatter | solution.py:240
  528.2 648.6 %reduce-scatter.14.cloned.1.call-start = ((), (), s32[]{:S(2)}) async-start(), calls=%async_computation.12 | async-start | bytes 9437184 | tf_op jit(solution)/shard_map/reduce_scatter | solution.py:241
  539.2 39.0 %copy-start.7 = (bf16[256,2048]{1,0:T(8,128)(2,1)S(1)}, bf16[256,2048]{1,0:T(8,128)(2,1)}, u32[]{:S(2)}) copy-start(bf16[256,2048]{1,0:T(8,128)(2,1)} %param.23) | copy-start | bytes 3145732
  539.2 79.6 %copy-start.14 = (bf16[256,2048]{1,0:T(8,128)(2,1)S(1)}, bf16[256,2048]{1,0:T(8,128)(2,1)}, u32[]{:S(2)}) copy-start(bf16[256,2048]{1,0:T(8,128)(2,1)} %param.38) | copy-start | bytes 3145732
  539.2 79.6 %copy-start.58 = (f32[256]{0:T(256)S(1)}, f32[256]{0:T(256)}, u32[]{:S(2)}) copy-start(f32[256]{0:T(256)} %get-tuple-element.522) | copy-start | bytes 3076
  (60 other events, 539.7 us)
Sparse Core Ops, SparseCore 0:
  12.1 37.1 all-gather.2
  50.9 34.4 all-gather.4
  418.7 90.2 reduce-scatter.9
  511.6 71.7 reduce-scatter.7
  587.1 61.2 reduce-scatter.17
  652.4 66.9 reduce-scatter.15
  723.5 148.3 reduce-scatter.19
  876.5 148.0 reduce-scatter.11
  1028.8 147.9 reduce-scatter.13
where the time goes:
time: 1200 us; the launch traced here: 1180 us
  waiting for transfers between devices  588 us (49%)
  matrix products  238 us (20%)
  blocking collectives  129 us (11%)
  local copies, waits for them, and re-layouts  109 us (9%)
  other arithmetic  102 us (8%)
  between operations  16.2 us (1%)
    reduce_scatter x1, waiting for transfers between devices, per_device(): lax.psum_scatter(gate_part, 'dp', scatter_dimension=0, tiled=True)  153 us
    reduce_scatter x1, waiting for transfers between devices, per_device(): lax.psum_scatter(out_proj_part, 'dp', scatter_dimension=1, tiled=True)  153 us
    reduce_scatter x1, waiting for transfers between devices, per_device(): lax.psum_scatter(value_part, 'dp', scatter_dimension=0, tiled=True)  152 us
    reduce_scatter x1, waiting for transfers between devices, per_device(): lax.psum_scatter(state_part, 'dp', scatter_dimension=0, tiled=True)  70.9 us
    dot_general x3, matrix products, state_space(): within = jnp.einsum('cijh,cjhp->cihp', mixing, scaled, precision=HIGH)  69.8 us
    psum x1, blocking collectives, per_device(): lax.psum((d_state_pre, g_conv_state, g_conv_state_bias), 'head')  42.1 us
    dot_general x5, matrix products, contract_rows(): lax.dot_general(left, right, (((0,), (0,)), ((), ())), preferred_element_...  39.8 us
    psum x1, blocking collectives, per_device(): lax.psum((g_conv_value, g_conv_value_bias, g_step_bias, g_decay_log, g_sk...  38 us
  transfers between devices with their start and end apart: 9, of which 6 were waited for; matrix products, arithmetic and copies ran while one was open for 18% of the time, Pallas kernels for 0%

commit v1 on v0

--- a/solution.py
+++ b/solution.py
@@ -117,7 +117,15 @@
     resid = hidden_in.astype(jnp.float32)
     in_scale = lax.rsqrt(jnp.mean(resid * resid, axis=-1, keepdims=True) + EPS)
     normed = (resid * in_scale * in_gain).astype(jnp.bfloat16)
-    whole = lax.all_gather(normed, "head", axis=0, tiled=True)
+    ways, here, lap = (lax.axis_size("head"), lax.axis_index("head"), normed.shape[0])
+    line, have = (normed, 1)
+    while have < ways:
+        line = jnp.concatenate(
+            [line, lax.ppermute(line, "head", [(d, (d - have) % ways) for d in range(ways)])],
+            axis=0,
+        )
+        have = 2 * have
+    whole = jnp.roll(line, here * lap, axis=0)
     rows_all = whole.shape[0]
     seq_len = rows_all // seqs
     gate_pre = jnp.dot(whole, gate_proj, preferred_element_type=jnp.float32)

time: 1200 us -> 1250 us (1.042)
  waiting for transfers between devices: 588 us -> 628 us
  local copies, waits for them, and re-layouts: 109 us -> 130 us
    ppermute x0 -> x2, waiting for transfers between devices: none -> 78.7 us  [per_device(): lax.ppermute(line, 'head', [(d, (d - have) % ways) for d in range(ways)])]
    all_gather x1 -> x0, waiting for transfers between devices: 33.9 us -> none  [per_device(): whole = lax.all_gather(normed, 'head', axis=0, tiled=True)]
  transfers between devices with their start and end apart: 9 -> 10, of which waited for: 6 -> 7; matrix products, arithmetic and copies ran while one was open for 18% -> 19% of each run, Pallas kernels for 0% -> 0%
where the time goes in v1:
time: 1250 us; the launch traced here: 1240 us
  waiting for transfers between devices  628 us (50%)
  matrix products  235 us (19%)
  local copies, waits for them, and re-layouts  130 us (10%)
  blocking collectives  129 us (10%)
  other arithmetic  101 us (8%)
  between operations  16.5 us (1%)
    reduce_scatter x1, waiting for transfers between devices, per_device(): lax.psum_scatter(gate_part, 'dp', scatter_dimension=0, tiled=True)  153 us
    reduce_scatter x1, waiting for transfers between devices, per_device(): lax.psum_scatter(out_proj_part, 'dp', scatter_dimension=1, tiled=True)  153 us
    reduce_scatter x1, waiting for transfers between devices, per_device(): lax.psum_scatter(value_part, 'dp', scatter_dimension=0, tiled=True)  152 us
    ppermute x2, waiting for transfers between devices, per_device(): lax.ppermute(line, 'head', [(d, (d - have) % ways) for d in range(ways)])  78.7 us
    reduce_scatter x1, waiting for transfers between devices, per_device(): lax.psum_scatter(state_part, 'dp', scatter_dimension=0, tiled=True)  70.8 us
    dot_general x3, matrix products, state_space(): within = jnp.einsum('cijh,cjhp->cihp', mixing, scaled, precision=HIGH)  70.4 us
    psum x1, blocking collectives, per_device(): lax.psum((d_state_pre, g_conv_state, g_conv_state_bias), 'head')  42.6 us
    dot_general x5, matrix products, contract_rows(): lax.dot_general(left, right, (((0,), (0,)), ((), ())), preferred_element_...  38.3 us
  transfers between devices with their start and end apart: 10, of which 7 were waited for; matrix products, arithmetic and copies ran while one was open for 19% of the time, Pallas kernels for 0%

profile of v1, /device:TPU:0, one launch (start us, length us, event | category | flops | bytes accessed | tf_op | source)
XLA Modules:
  0.0 1243.1 jit_solution(5880778794831494170)
XLA Ops:
  14.4 12.3 collective-permute-done
  33.2 66.4 %collective-permute-done.1 = bf16[512,2048]{1,0:T(8,128)(2,1)} collective-permute-done((bf16[512,2048]{1,0:T(8,128)(2,1)}, bf16[512,2048]{1,0:T(8,128)(2,1)}, u32[]{:S(2)}, u32[]{:S(2)}) %collective-permute-start.1) | collective-permute-done | bytes 2097184 | tf_op jit(solution)/shard_map/ppermute | solution.py:124
  184.1 21.2 %fusion.9 = f32[4,16,64,256]{3,2,1,0:T(8,128)S(1)} fusion(f32[4,256,256]{2,1,0:T(8,128)S(1)} %fusion.153, f32[4,256,16]{1,2,0:T(8,128)S(1)} %get-tuple-element.534, pred[256,256]{1,0:T(8,128)(4,1)} %iota_compare_fusion, f32[4,256,16,64]{1,3,2,0:T(8,128)} %copy.274, f32[4,256,16]{1,2,0:T(8,128)S(1)} %bitcast.311, f32[16]{0:T(128)S(1)} %compare_convert_fusion), kind=kOutput, calls=%fused_computation.25 | convolution fusion | flops 3240099840 | bytes 9633856 | tf_op jit(solution)/shard_map/vmap(cijh,cjhp->cihp)/dot_general | solution.py:34
  228.9 12.7 %multiply_reduce_fusion.8 = (f32[1024]{0:T(1024)S(1)}, f32[1024,1024]{1,0:T(8,128)}, f32[1024,1024]{1,0:T(8,128)}) fusion(f32[1024,1024]{1,0:T(8,128)} %reshape.750, bf16[2048,1024]{1,0:T(8,128)(2,1)} %param.25, bf16[2048,2048]{1,0:T(8,128)(2,1)} %constant_dynamic-update-slice_fusion.2, s32[]{:T(128)S(6)} %select_n.81), kind=kOutput, calls=%fused_computation.79 | convolution fusion | flops 4302306304 | bytes 20975620 | tf_op jit(solution)/shard_map/dot_general | solution.py:131
  249.0 10.4 while.48
  259.4 11.9 multiply_reduce_fusion
  276.9 9.7 fusion.28
  303.3 29.0 %fusion.11 = (f32[4,256,16]{1,2,0:T(8,128)S(1)}, f32[4,256,16]{1,2,0:T(8,128)S(1)}, f32[4,256,256]{2,1,0:T(8,128)}) fusion(f32[4,256,16]{1,2,0:T(8,128)} %copy-done.36, f32[4,256,256]{2,1,0:T(8,128)S(1)} %copy-done.28, pred[256,256]{1,0:T(8,128)(4,1)} %iota_compare_fusion, f32[4,256,16,64]{1,3,2,0:T(8,128)} %copy.274, f32[4,256,16]{1,2,0:T(8,128)S(1)} %bitcast.312, ...), kind=kOutput, calls=%fused_computation.27 | convolution fusion | flops 3269165056 | bytes 10813504 | tf_op jit(solution)/shard_map/transpose(jvp(vmap(cijh,cjhp->cihp)))/dot_general | solution.py:34
  344.9 11.8 while.49
  362.3 20.3 %fusion.29 = (f32[4,256,16]{1,2,0:T(8,128)S(1)}, f32[4,256,16]{1,2,0:T(8,128)S(1)}, f32[1,4,256,16,64]{2,4,3,1,0:T(8,128)}, f32[1,4,256,16,64]{2,4,3,1,0:T(8,128)}) fusion(f32[4,16,64,256]{3,2,1,0:T(8,128)S(1)} %fusion.56, f32[1,4,256,16,64]{2,4,3,1,0:T(8,128)S(1)} %copy-done.7, f32[4,256,16]{1,2,0:T(8,128)S(1)} %bitcast.313, f32[16]{0:T(128)S(1)} %copy-done.64, ...), kind=kOutput, calls=%fused_computation.61 | convolution fusion | flops 3253698560 | bytes 35061888 | tf_op jit(solution)/shard_map/transpose(jvp(vmap(cijh,cjhp->cihp)))/dot_general | solution.py:34
  383.5 9.9 reduce-window.16
  409.8 12.1 multiply_reduce_fusion.3
  477.5 13.0 %fusion.141 = f32[1024,2048]{1,0:T(8,128)} fusion(bf16[1024,2048]{1,0:T(8,128)(2,1)} %param.37, f32[1024,1024]{1,0:T(8,128)} %get-tuple-element.489, f32[1024]{0:T(1024)S(1)} %copy-done.30, f32[1024]{0:T(1024)S(1)} %get-tuple-element.487), kind=kOutput, calls=%fused_computation.237 | convolution fusion | flops 4298113024 | bytes 16785408 | tf_op jit(solution)/shard_map/dot_general | solution.py:167
  518.6 42.6 %all-reduce.25 = (bf16[1024,256]{1,0:T(8,128)(2,1)S(1)}, f32[4,256]{1,0:T(4,128)S(1)}, f32[256]{0:T(256)S(1)}) all-reduce(f32[1024,256]{1,0:T(8,128)S(1)} %fusion.95, f32[4,256]{1,0:T(4,128)S(1)} %pad_add_fusion.7, f32[256]{0:T(256)S(1)} %get-tuple-element.429), channel_id=1, replica_groups=mesh['dp'=8,'head'=4] {'head'}, use_global_device_ids=true, to_apply=%region_25.26 | all-reduce | flops 263424 | bytes 1583104 | tf_op jit(solution)/shard_map/psum | solution.py:194
  566.7 12.4 fusion.140
  581.1 9.9 fusion.105
  592.6 9.6 fusion.103
  603.1 38.0 %all-reduce.22 = (f32[4,1024]{1,0:T(4,128)}, f32[1024]{0:T(1024)}, f32[4,256]{1,0:T(4,128)}, f32[256]{0:T(256)}, f32[16]{0:T(128)}, /*index=5*/f32[16]{0:T(128)}, f32[16]{0:T(128)}, f32[1024]{0:T(1024)}) all-reduce(f32[4,1024]{1,0:T(4,128)S(1)} %pad_add_fusion.6, ...), channel_id=1, replica_groups=mesh['dp'=8,'head'=4] {'dp'}, use_global_device_ids=true, to_apply=%region_37.38 | all-reduce | flops 7472 | bytes 59776 | tf_op jit(solution)/shard_map/psum | solution.py:234
  645.0 36.9 %psum.101 = f32[2048]{0:T(1024)} all-reduce(f32[2048]{0:T(1024)S(1)} %get-tuple-element.424), channel_id=1, replica_groups=mesh['dp'=8,'head'=4] {'dp','head'}, use_global_device_ids=true, to_apply=%region_28.29 | all-reduce | flops 2048 | bytes 16384 | tf_op jit(solution)/shard_map/psum | solution.py:224
  686.6 20.9 %reduce-scatter.18.cloned.1.call-done = f32[256,16]{0,1:T(8,128)} async-done(((f32[2048,16]{0,1:T(8,128)}), f32[256,16]{0,1:T(8,128)}) %reduce-scatter.18.cloned.1.call-update) | async-done | bytes 16400 | tf_op jit(solution)/shard_map/reduce_scatter | solution.py:251
  707.5 70.8 %reduce-scatter.16.cloned.1.call-done = f32[256,256]{1,0:T(8,128)} async-done(((f32[2048,256]{1,0:T(8,128)}), f32[256,256]{1,0:T(8,128)}) %reduce-scatter.16.cloned.1.call-update) | async-done | bytes 262160 | tf_op jit(solution)/shard_map/reduce_scatter | solution.py:250
  778.3 152.5 %reduce-scatter.20.cloned.1.call-done = f32[1024,256]{1,0:T(8,128)} async-done(((f32[1024,2048]{1,0:T(8,128)}), f32[1024,256]{1,0:T(8,128)}) %reduce-scatter.20.cloned.1.call-update) | async-done | bytes 1048592 | tf_op jit(solution)/shard_map/reduce_scatter | solution.py:252
  930.9 152.7 %reduce-scatter.12.cloned.1.call-done = f32[256,1024]{1,0:T(8,128)} async-done(((f32[2048,1024]{1,0:T(8,128)}), f32[256,1024]{1,0:T(8,128)}) %reduce-scatter.12.cloned.1.call-update) | async-done | bytes 1048592 | tf_op jit(solution)/shard_map/reduce_scatter | solution.py:248
  1083.5 152.3 %reduce-scatter.14.cloned.1.call-done = f32[256,1024]{1,0:T(8,128)} async-done(((f32[2048,1024]{1,0:T(8,128)}), f32[256,1024]{1,0:T(8,128)}) %reduce-scatter.14.cloned.1.call-update) | async-done | bytes 1048592 | tf_op jit(solution)/shard_map/reduce_scatter | solution.py:249
  (348 shorter events, 317.5 us)
Async XLA Ops:
  7.2 135.8 %copy-start = (bf16[2048,256]{1,0:T(8,128)(2,1)S(1)}, bf16[2048,256]{1,0:T(8,128)(2,1)}, u32[]{:S(2)}) copy-start(bf16[2048,256]{1,0:T(8,128)(2,1)} %param.27) | copy-start | bytes 3145732
  7.2 252.2 %all-gather.2.cloned.1.call-start = ((), (), s32[]{:S(2)}) async-start(), calls=%async_computation.8 | async-start | bytes 5242880 | tf_op jit(solution)/shard_map/all_gather | solution.py:173
  12.0 14.7 %collective-permute-start = (bf16[256,2048]{1,0:T(8,128)(2,1)S(1)}, bf16[256,2048]{1,0:T(8,128)(2,1)S(1)}, u32[]{:S(2)}, u32[]{:S(2)}) collective-permute-start(bf16[256,2048]{1,0:T(8,128)(2,1)S(1)} %get-tuple-element.497), channel_id=1, source_target_pairs={{0,3},{1,0},{2,1},{3,2},{4,7},{5,4},{6,5},{7,6},{8,11},{9,8},{10,9... | collective-permute-start | bytes 3145736 | tf_op jit(solution)/shard_map/ppermute | solution.py:124
  28.4 71.2 %collective-permute-start.1 = (bf16[512,2048]{1,0:T(8,128)(2,1)}, bf16[512,2048]{1,0:T(8,128)(2,1)}, u32[]{:S(2)}, u32[]{:S(2)}) collective-permute-start(bf16[512,2048]{1,0:T(8,128)(2,1)} %pad_maximum_fusion), channel_id=1, source_target_pairs={{0,2},{1,3},{2,0},{3,1},{4,6},{5,7},{6,4},{7,5},{8,10},{9,11},{10,... | collective-permute-start | bytes 6291464 | tf_op jit(solution)/shard_map/ppermute | solution.py:124
  29.0 612.2 %reduce-scatter.10.cloned.1.call-start = ((), (), s32[]{:S(2)}) async-start(), calls=%async_computation.9 | async-start | bytes 10485760 | tf_op jit(solution)/shard_map/reduce_scatter | solution.py:201
  29.8 175.5 %copy-start.63 = (f32[16]{0:T(128)}, f32[16]{0:T(128)S(1)}, u32[]{:S(2)}) copy-start(f32[16]{0:T(128)S(1)} %compare_convert_fusion) | copy-start | bytes 196
  30.6 81.4 %copy-start.70 = (f32[16]{0:T(128)}, f32[16]{0:T(128)S(1)}, u32[]{:S(2)}) copy-start(f32[16]{0:T(128)S(1)} %exponential_negate_fusion) | copy-start | bytes 196
  30.6 115.9 %copy-start.55 = (f32[1,256]{1,0:T(1,128)}, f32[1,256]{1,0:T(1,128)S(1)}, u32[]{:S(2)}) copy-start(f32[1,256]{1,0:T(1,128)S(1)} %get-tuple-element.520) | copy-start | bytes 3076
  30.6 115.9 %copy-start.57 = (f32[1,256]{1,0:T(1,128)}, f32[1,256]{1,0:T(1,128)S(1)}, u32[]{:S(2)}) copy-start(f32[1,256]{1,0:T(1,128)S(1)} %get-tuple-element.521) | copy-start | bytes 3076
  30.6 115.9 %copy-start.59 = (f32[1,256]{1,0:T(1,128)}, f32[1,256]{1,0:T(1,128)S(1)}, u32[]{:S(2)}) copy-start(f32[1,256]{1,0:T(1,128)S(1)} %get-tuple-element.522) | copy-start | bytes 3076
  30.6 115.9 %copy-start.61 = (f32[1,256]{1,0:T(1,128)}, f32[1,256]{1,0:T(1,128)S(1)}, u32[]{:S(2)}) copy-start(f32[1,256]{1,0:T(1,128)S(1)} %get-tuple-element.523) | copy-start | bytes 3076
  30.7 91.5 %copy-start.38 = (f32[1,1024]{1,0:T(1,128)}, f32[1,1024]{1,0:T(1,128)S(1)}, u32[]{:S(2)}) copy-start(f32[1,1024]{1,0:T(1,128)S(1)} %get-tuple-element.516) | copy-start | bytes 12292
  30.7 91.5 %copy-start.40 = (f32[1,1024]{1,0:T(1,128)}, f32[1,1024]{1,0:T(1,128)S(1)}, u32[]{:S(2)}) copy-start(f32[1,1024]{1,0:T(1,128)S(1)} %get-tuple-element.517) | copy-start | bytes 12292
  30.7 91.5 %copy-start.42 = (f32[1,1024]{1,0:T(1,128)}, f32[1,1024]{1,0:T(1,128)S(1)}, u32[]{:S(2)}) copy-start(f32[1,1024]{1,0:T(1,128)S(1)} %get-tuple-element.518) | copy-start | bytes 12292
  30.7 91.5 %copy-start.44 = (f32[1,1024]{1,0:T(1,128)}, f32[1,1024]{1,0:T(1,128)S(1)}, u32[]{:S(2)}) copy-start(f32[1,1024]{1,0:T(1,128)S(1)} %get-tuple-element.519) | copy-start | bytes 12292
  30.7 73.0 %copy-start.16 = (bf16[256,2048]{1,0:T(8,128)(2,1)S(1)}, bf16[256,2048]{1,0:T(8,128)(2,1)}, u32[]{:S(2)}) copy-start(bf16[256,2048]{1,0:T(8,128)(2,1)} %copy-done.15) | copy-start | bytes 3145732
  477.2 204.7 %reduce-scatter.8.cloned.1.call-start = ((), (), s32[]{:S(2)}) async-start(), calls=%async_computation.7 | async-start | bytes 10485760 | tf_op jit(solution)/shard_map/reduce_scatter | solution.py:166
  490.5 217.0 %reduce-scatter.18.cloned.1.call-start = ((), (), s32[]{:S(2)}) async-start(), calls=%async_computation.13 | async-start | bytes 147456 | tf_op jit(solution)/shard_map/reduce_scatter | solution.py:251
  518.5 259.8 %reduce-scatter.16.cloned.1.call-start = ((), (), s32[]{:S(2)}) async-start(), calls=%async_computation.12 | async-start | bytes 2359296 | tf_op jit(solution)/shard_map/reduce_scatter | solution.py:250
  566.4 364.5 %reduce-scatter.20.cloned.1.call-start = ((), (), s32[]{:S(2)}) async-start(), calls=%async_computation.14 | async-start | bytes 9437184 | tf_op jit(solution)/shard_map/reduce_scatter | solution.py:252
  579.1 504.5 %reduce-scatter.12.cloned.1.call-start = ((), (), s32[]{:S(2)}) async-start(), calls=%async_computation.10 | async-start | bytes 9437184 | tf_op jit(solution)/shard_map/reduce_scatter | solution.py:248
  591.0 644.8 %reduce-scatter.14.cloned.1.call-start = ((), (), s32[]{:S(2)}) async-start(), calls=%async_computation.11 | async-start | bytes 9437184 | tf_op jit(solution)/shard_map/reduce_scatter | solution.py:249
  602.2 79.7 %copy-start.18 = (bf16[256,2048]{1,0:T(8,128)(2,1)S(1)}, bf16[256,2048]{1,0:T(8,128)(2,1)}, u32[]{:S(2)}) copy-start(bf16[256,2048]{1,0:T(8,128)(2,1)} %param.38) | copy-start | bytes 3145732
  602.3 79.7 %copy-start.66 = (f32[256]{0:T(256)S(1)}, f32[256]{0:T(256)}, u32[]{:S(2)}) copy-start(f32[256]{0:T(256)} %get-tuple-element.524) | copy-start | bytes 3076
  (70 other events, 764.9 us)
Sparse Core Ops, SparseCore 0:
  29.1 58.4 all-gather.1
  477.4 90.5 reduce-scatter.9
  570.7 71.7 reduce-scatter.7
  646.2 61.2 reduce-scatter.17
  711.5 66.8 reduce-scatter.15
  782.4 148.4 reduce-scatter.19
  935.5 147.9 reduce-scatter.11
  1087.7 148.0 reduce-scatter.13
